TPU v7x, 32 devices: a whole 2x2x4 slice. The times are simulated.
32 devices in a mesh: gz: 8 (over z, y), gy: 4 (over x, core).
Axes of the slice: x: 2, y: 2, z: 4, core: 2. Of those that a mesh axis runs over, the one named last changes fastest.
Arguments:
- velocity: float32 [2, 6, 1024, 2048], P(None, None, 'gy', 'gz'), may hold values from -6 to 6
Outputs:
- spectrum: float32 [2, 6, 1024, 2048], P(None, None, 'gy', 'gz')
All inputs are finite; a program needn't handle non-finite values.
Results may differ from a plain program's by a relative error of at most 0.000098.
Values sent between devices are 32-bit elements; how exact they have to be, the bound alone decides.
No kernel may reach another device: no remote copies, remote signals or barrier semaphores. Data moves between devices by JAX's collectives and lax.ppermute only.
A program may use at most 64 MiB of HBM per device.

v0:
```python
import functools
import math

import jax
import jax.numpy as jnp
import numpy as np
from jax import lax
from jax.experimental import pallas as pl
from jax.experimental.pallas import tpu as pltpu
from jax.sharding import PartitionSpec as P


GRANT = 16 * 2**20

F32 = jnp.float32
BF16 = jnp.bfloat16
SMEM = pl.BlockSpec(memory_space=pltpu.SMEM)
VMEM = pl.BlockSpec(memory_space=pltpu.VMEM)
ANY = pl.BlockSpec(memory_space=pl.ANY)


def exchanged(block, axis, mask):
    count = lax.axis_size(axis)
    return lax.ppermute(block, axis, [(i, i ^ mask) for i in range(count)])


def reversed_bits(index, bit_count):
    return sum(((index >> place) & 1) << (bit_count - 1 - place) for place in range(bit_count))


def unit(products, length):
    phase = -2.0 * math.pi * (products % length).astype(F32) / length
    return jnp.cos(phase), jnp.sin(phase)


def estimate(flops, count):
    return pl.CostEstimate(flops=flops, transcendentals=0, bytes_accessed=4 * count)


def dft_matrix(frequency, count, local, at):
    length = count * local
    to = jnp.arange(local, dtype=jnp.int32)
    cosine, sine = unit(at[:, None] * (frequency + count * to[None, :]), length)
    scale = 1.0 / math.sqrt(length)
    return cosine * scale, sine * scale


def split(values):
    high = lax.reduce_precision(values, 8, 7)
    return jnp.stack([high.astype(BF16), (values - high).astype(BF16)])


def right_matrix(frequency, count, local):
    cosine, sine = dft_matrix(frequency, count, local, jnp.arange(local, dtype=jnp.int32))
    return split(jnp.block([[cosine, sine], [-sine, cosine]]))


def left_matrix(frequency, count, local, part):
    at = jnp.arange(local, dtype=jnp.int32)
    quarter = local // 4
    at = (part ^ (at // quarter)) * quarter + at % quarter
    cosine, sine = dft_matrix(frequency, count, local, at)
    return split(jnp.block([[cosine.T, -sine.T], [sine.T, cosine.T]]))


def halves(values):
    high = values.astype(BF16)
    return high, (values - high.astype(F32)).astype(BF16)


def dot3(left, right):
    def single(a, b):
        return jnp.dot(a, b, preferred_element_type=F32)

    return single(left[0], right[0]) + (single(left[1], right[0]) + single(left[0], right[1]))


def along_last(real, imag, matrix_ref):
    local = real.shape[-1]
    mixed = dot3(halves(jnp.concatenate([real, imag], axis=1)), (matrix_ref[0], matrix_ref[1]))
    return mixed[:, :local], mixed[:, local:]


def along_first(real, imag, matrix_ref):
    local = real.shape[0]
    mixed = dot3((matrix_ref[0], matrix_ref[1]), halves(jnp.concatenate([real, imag], axis=0)))
    return mixed[:local], mixed[local:]


def after(value, done):
    return value if done is None else lax.optimization_barrier((value, done))[0]


def turned(values, cosine, sine):
    real, imag = values[:, :1], values[:, 1:]
    return jnp.concatenate([real * cosine - imag * sine, real * sine + imag * cosine], axis=1)


def butterfly(own, other, pair, bit):
    both = own * pair[0] + other
    return turned(both, pair[1], pair[2]) if bit else both


def per_rows(planes, rows, step, body):
    def one(at, carry):
        body(at // (rows // step), pl.multiple_of(at % (rows // step) * step, step))
        return carry

    lax.fori_loop(0, planes * (rows // step), one, 0, unroll=4)


def mix_kernel(coef_ref, *refs):
    pieces, outs = refs[:4], refs[4:]
    planes, half = outs[0].shape[2:4]
    for h, out_ref in enumerate(outs):

        def body(plane, at, h=h, out_ref=out_ref):
            rows = pl.ds(h * half + at, 8)
            values = [(ref[0, plane, rows, :], ref[1, plane, rows, :]) for ref in pieces]
            for e in range(4):
                real, imag = None, None
                for d in range(4):
                    c, s = coef_ref[4 * e + d], coef_ref[16 + 4 * e + d]
                    a, b = values[d]
                    re, im = a * c - b * s, a * s + b * c
                    real = re if real is None else real + re
                    imag = im if imag is None else imag + im
                out_ref[e, 0, plane, pl.ds(at, 8), :] = real
                out_ref[e, 1, plane, pl.ds(at, 8), :] = imag

        per_rows(planes, half, 8, body)


def mix(pieces, coefs):
    _, planes, quarter, columns = pieces[0].shape
    half = jax.ShapeDtypeStruct((4, 2, planes, quarter // 2, columns), F32)
    return pl.pallas_call(
        mix_kernel,
        in_specs=[SMEM] + [VMEM] * 4,
        out_specs=[VMEM] * 2,
        out_shape=[half] * 2,
        compiler_params=pltpu.CompilerParams(vmem_limit_bytes=GRANT),
        cost_estimate=estimate(128 * planes * quarter * columns, 16 * planes * quarter * columns),
        name="mix",
    )(coefs, *pieces)


def join_kernel(twist, coef_ref, *refs):
    sides, outs = (refs[0:2], refs[2:4]), refs[4:]
    groups, _, planes, half, _ = refs[0].shape
    flip = coef_ref[0]
    for h, (own_ref, other_ref) in enumerate(sides):

        def body(plane, at, h=h, own_ref=own_ref, other_ref=other_ref):
            rows, into = pl.ds(at, 8), pl.ds(h * half + at, 8)
            for e in range(groups):
                real, imag = [own_ref[e, p, plane, rows, :] * flip + other_ref[e, p, plane, rows, :] for p in range(2)]
                if twist:
                    real, imag = real * coef_ref[1] - imag * coef_ref[2], real * coef_ref[2] + imag * coef_ref[1]
                outs[e][0, plane, into, :] = real
                outs[e][1, plane, into, :] = imag

        per_rows(planes, half, 8, body)


def join(own, other, pair, bit):
    groups, _, planes, half, columns = own[0].shape
    piece = jax.ShapeDtypeStruct((2, planes, 2 * half, columns), F32)
    return pl.pallas_call(
        functools.partial(join_kernel, bit > 0),
        in_specs=[SMEM] + [VMEM] * 4,
        out_specs=[VMEM] * groups,
        out_shape=[piece] * groups,
        compiler_params=pltpu.CompilerParams(vmem_limit_bytes=GRANT),
        cost_estimate=estimate(10 * own[0].size, 6 * own[0].size),
        name="join",
    )(pair, own[0], other[0], own[1], other[1])


def finish_kernel(start, right_ref, left_ref, e0_ref, e1_ref, e2_ref, e3_ref, *rest):
    out_ref, done, sems = rest[-3:]
    planes = e0_ref.shape[1]
    copies = []
    for plane in range(planes):
        refs = (e0_ref, e1_ref, e2_ref, e3_ref)
        whole = [jnp.concatenate([ref[part, plane] for ref in refs], axis=0) for part in range(2)]
        real, imag = along_last(whole[0], whole[1], right_ref)
        real, imag = along_first(real, imag, left_ref)
        done[plane, 0] = real
        done[plane, 1] = imag
        copies.append(pltpu.make_async_copy(done.at[plane], out_ref.at[:, start + plane], sems.at[plane]))
        copies[-1].start()
    for copy in copies:
        copy.wait()


def finish(pieces, right, left, out, start, total):
    _, planes, quarter, columns = pieces[0].shape
    rows = 4 * quarter
    in_specs = [VMEM] * 6
    args = [right, left, *pieces]
    aliases = {}
    if out is not None:
        in_specs.append(ANY)
        aliases = {len(args): 0}
        args.append(out)
    return pl.pallas_call(
        functools.partial(finish_kernel, start),
        in_specs=in_specs,
        out_specs=ANY,
        out_shape=jax.ShapeDtypeStruct((2, total, rows, columns), F32),
        scratch_shapes=[
            pltpu.VMEM((planes, 2, rows, columns), F32),
            pltpu.SemaphoreType.DMA((planes,)),
        ],
        input_output_aliases=aliases,
        compiler_params=pltpu.CompilerParams(vmem_limit_bytes=GRANT),
        cost_estimate=estimate(24 * planes * rows * columns * (rows + columns), 4 * planes * rows * columns),
        name="finish",
    )(*args)


def host_unit(products, length):
    value = np.exp(-2j * np.pi * (np.asarray(products) % length) / length)
    return value.real, value.imag


def pair_table(count, bit):
    index = np.arange(count)
    upper = (index >> bit) & 1
    return np.stack([1 - 2 * upper, *host_unit((index % 2**bit) * upper, 2 ** (bit + 1))], axis=1)


def mix_table(count):
    index, step = np.arange(count), np.arange(4)
    part, rest = index // (count // 4), index % (count // 4)
    k = reversed_bits(part[:, None] ^ step, 2)[:, :, None]
    d = (part[:, None] ^ step)[:, None, :]
    cosine, sine = host_unit(rest[:, None, None] * k + (count // 4) * (d * k), count)
    return np.concatenate([cosine.reshape(count, 16), sine.reshape(count, 16)], axis=1)


def row_of(table, index):
    table = jnp.asarray(table, F32)
    row = lax.dynamic_slice(table, (index, jnp.uint32(0)), (1, table.shape[1]))
    return row.reshape(table.shape[1])


def chunks_of(planes):
    size = max(1, planes // 3)
    starts = list(range(0, planes, size))
    return [(at, min(size, planes - at)) for at in starts]


def order_of(chunks, steps):
    sizes = [size / chunks[0][1] for _, size in chunks]
    ready, at, free, order = [], 0.5, 0.0, []
    for i, size in enumerate(sizes):
        at += size
        ready.append((at, i, 0))
    while ready:
        ready.sort()
        now, i, step = ready.pop(0)
        order.append((i, step))
        if step < steps - 2:
            free = max(now + 0.1, free) + sizes[i] / 2
            ready.append((free, i, step + 1))
        elif step < steps - 1:
            ready.append((now + 0.1, i, step + 1))
    return order


def shards(velocity):
    _, planes, rows, columns = velocity.shape
    z_count = lax.axis_size("gz")
    y_count = lax.axis_size("gy")
    z_bits = z_count.bit_length() - 1
    y_bits = y_count.bit_length() - 1
    stride = z_count // 4
    quarter = rows // 4
    z_index = lax.axis_index("gz").astype(jnp.uint32)
    y_index = lax.axis_index("gy").astype(jnp.uint32)
    part = z_index >> (z_bits - 2)
    peers = [part ^ d for d in range(4)]
    shifts = [reversed_bits(z_index, z_bits), reversed_bits(y_index, y_bits)]
    velocity, z_index, y_index, part, peers, shifts = lax.optimization_barrier(
        (velocity, z_index, y_index, part, peers, shifts)
    )

    chunks = chunks_of(planes)
    quarters = velocity.reshape(2, planes, 4, quarter, columns)
    received = []
    zero = jnp.uint32(0)
    for start, size in chunks:
        shape = (2, size, 1, quarter, columns)
        at = jnp.uint32(start)
        pieces = [lax.dynamic_slice(quarters, (zero, at, peer, zero, zero), shape)[:, :, 0] for peer in peers]
        quarters = after(quarters, pieces)
        received.append(pieces[:1] + [exchanged(pieces[d], "gz", d * stride) for d in range(1, 4)])

    coefs = row_of(mix_table(z_count), z_index)
    right = right_matrix(shifts[0].astype(jnp.int32), z_count, columns)
    left = left_matrix(shifts[1].astype(jnp.int32), y_count, rows, part.astype(jnp.int32))
    z_pairs = [("gz", bit, row_of(pair_table(z_count, bit), z_index)) for bit in reversed(range(z_bits - 2))]
    y_pairs = [("gy", bit, row_of(pair_table(y_count, bit), y_index)) for bit in reversed(range(y_bits))]
    ways = list(zip(z_pairs + y_pairs[:-1], y_pairs[:-1] + z_pairs))
    ways.append((y_pairs[-1], y_pairs[-1]))

    state = [None] * len(chunks)
    done = None
    steps = len(ways) + 1
    back = [None] * len(chunks)
    for i, step in order_of(chunks, steps):
        if step == 0:
            pieces = after(received[i], done)
            state[i] = mix(pieces, coefs)
        else:
            way = ways[step - 1]
            other = [exchanged(block, axis, 2**bit) for block, (axis, bit, _) in zip(state[i], way)]
            own, other = after((state[i], other), done)
            if step == steps - 1:
                pieces = list(join(own, other, way[0][2], way[0][1]))
            else:
                pieces = [butterfly(a, b, pair, bit) for a, b, (_, bit, pair) in zip(own, other, way)]
            state[i] = pieces
            if step == steps - 1:
                back[i] = pieces[:1] + [exchanged(pieces[d], "gz", d * stride) for d in range(1, 4)]
        done = state[i]
    result = None
    for i, (start, _) in enumerate(chunks):
        result = finish(back[i], right, left, result, start, planes)
    return result


def solution(mesh):
    in_specs = (P(None, None, "gy", "gz"),)
    out_specs = P(None, None, "gy", "gz")
    return jax.shard_map(shards, mesh=mesh, in_specs=in_specs, out_specs=out_specs, check_vma=False)
```

profile of v0, /device:TPU:19, one launch (start us, length us, event | category | flops | bytes accessed | tf_op | source)
XLA Modules:
  0.0 226.0 jit_solution(2504766684085480017)
XLA Ops:
  1.5 3.2 %collective-permute-start.7 = (f32[2,2,64,256]{3,2,1,0:T(8,128)S(1)}, f32[2,2,64,256]{3,2,1,0:T(8,128)S(1)}, u32[]{:S(2)}, u32[]{:S(2)}) collective-permute-start(f32[2,2,64,256]{3,2,1,0:T(8,128)S(1)} %get-tuple-element.162), channel_id=1, source_target_pairs={{0,16},{4,20},{8,24},{12,28},{16,0},{20,4},{24,8},{28,12},{1,17},{... | collective-permute-start | bytes 786440 | tf_op jit(solution)/shard_map/ppermute | solution.py:24
  5.4 14.4 %collective-permute-done.8.refs_3_ = f32[2,2,64,256]{3,2,1,0:T(8,128)S(1)} collective-permute-done((f32[2,2,64,256]{3,2,1,0:T(8,128)S(1)}, f32[2,2,64,256]{3,2,1,0:T(8,128)S(1)}, u32[]{:S(2)}, u32[]{:S(2)}) %collective-permute-start.8) | collective-permute-done | bytes 262176 | tf_op jit(solution)/shard_map/ppermute | solution.py:24
  19.8 3.8 %collective-permute-done.7.refs_2_ = f32[2,2,64,256]{3,2,1,0:T(8,128)S(1)} collective-permute-done((f32[2,2,64,256]{3,2,1,0:T(8,128)S(1)}, f32[2,2,64,256]{3,2,1,0:T(8,128)S(1)}, u32[]{:S(2)}, u32[]{:S(2)}) %collective-permute-start.7) | collective-permute-done | bytes 262176 | tf_op jit(solution)/shard_map/ppermute | solution.py:24
  24.7 1.3 collective-permute-start.9
  27.6 9.3 %collective-permute-done.9 = f32[4,2,2,32,256]{4,3,2,1,0:T(8,128)S(1)} collective-permute-done((f32[4,2,2,32,256]{4,3,2,1,0:T(8,128)S(1)}, f32[4,2,2,32,256]{4,3,2,1,0:T(8,128)S(1)}, u32[]{:S(2)}, u32[]{:S(2)}) %collective-permute-start.9) | collective-permute-done | bytes 524320 | tf_op jit(solution)/shard_map/ppermute | solution.py:24
  41.7 4.0 %collective-permute-start.4 = (f32[2,2,64,256]{3,2,1,0:T(8,128)S(1)}, f32[2,2,64,256]{3,2,1,0:T(8,128)S(1)}, u32[]{:S(2)}, u32[]{:S(2)}) collective-permute-start(f32[2,2,64,256]{3,2,1,0:T(8,128)S(1)} %get-tuple-element.158), channel_id=1, source_target_pairs={{0,16},{4,20},{8,24},{12,28},{16,0},{20,4},{24,8},{28,12},{1,17},{... | collective-permute-start | bytes 786440 | tf_op jit(solution)/shard_map/ppermute | solution.py:24
  46.3 15.9 %collective-permute-done.4.refs_2_ = f32[2,2,64,256]{3,2,1,0:T(8,128)S(1)} collective-permute-done((f32[2,2,64,256]{3,2,1,0:T(8,128)S(1)}, f32[2,2,64,256]{3,2,1,0:T(8,128)S(1)}, u32[]{:S(2)}, u32[]{:S(2)}) %collective-permute-start.4) | collective-permute-done | bytes 262176 | tf_op jit(solution)/shard_map/ppermute | solution.py:24
  64.0 1.3 multiply_subtract_fusion.4
  65.4 3.2 %collective-permute-start.16 = (f32[4,2,2,32,256]{4,3,2,1,0:T(8,128)S(1)}, f32[4,2,2,32,256]{4,3,2,1,0:T(8,128)S(1)}, u32[]{:S(2)}, u32[]{:S(2)}) collective-permute-start(f32[4,2,2,32,256]{4,3,2,1,0:T(8,128)S(1)} %multiply_add_fusion.8.refs_2_), channel_id=1, source_target_pairs={{0,1},{1,0},{2,3},{3,2},{4,5},{5,4},{6,7},{7,6},{8,9},{9,8},{10,11... | collective-permute-start | bytes 1572872 | tf_op jit(solution)/shard_map/ppermute | solution.py:24
  72.7 9.2 %collective-permute-done.11 = f32[4,2,2,32,256]{4,3,2,1,0:T(8,128)S(1)} collective-permute-done((f32[4,2,2,32,256]{4,3,2,1,0:T(8,128)S(1)}, f32[4,2,2,32,256]{4,3,2,1,0:T(8,128)S(1)}, u32[]{:S(2)}, u32[]{:S(2)}) %collective-permute-start.11) | collective-permute-done | bytes 524320 | tf_op jit(solution)/shard_map/ppermute | solution.py:24
  85.2 1.3 collective-permute-start.19
  87.6 4.0 %collective-permute-start.1 = (f32[2,2,64,256]{3,2,1,0:T(8,128)S(1)}, f32[2,2,64,256]{3,2,1,0:T(8,128)S(1)}, u32[]{:S(2)}, u32[]{:S(2)}) collective-permute-start(f32[2,2,64,256]{3,2,1,0:T(8,128)S(1)} %get-tuple-element.154), channel_id=1, source_target_pairs={{0,16},{4,20},{8,24},{12,28},{16,0},{20,4},{24,8},{28,12},{1,17},{... | collective-permute-start | bytes 786440 | tf_op jit(solution)/shard_map/ppermute | solution.py:24
  92.4 15.8 %collective-permute-done.1.refs_2_ = f32[2,2,64,256]{3,2,1,0:T(8,128)S(1)} collective-permute-done((f32[2,2,64,256]{3,2,1,0:T(8,128)S(1)}, f32[2,2,64,256]{3,2,1,0:T(8,128)S(1)}, u32[]{:S(2)}, u32[]{:S(2)}) %collective-permute-start.1) | collective-permute-done | bytes 262176 | tf_op jit(solution)/shard_map/ppermute | solution.py:24
  111.3 2.9 %collective-permute-start.22 = (f32[4,2,2,32,256]{4,3,2,1,0:T(8,128)S(1)}, f32[4,2,2,32,256]{4,3,2,1,0:T(8,128)S(1)}, u32[]{:S(2)}, u32[]{:S(2)}) collective-permute-start(f32[4,2,2,32,256]{4,3,2,1,0:T(8,128)S(1)} %multiply_add_fusion.4.refs_2_), channel_id=1, source_target_pairs={{0,1},{1,0},{2,3},{3,2},{4,5},{5,4},{6,7},{7,6},{8,9},{9,8},{10,11... | collective-permute-start | bytes 1572872 | tf_op jit(solution)/shard_map/ppermute | solution.py:24
  117.4 10.3 %collective-permute-done.17 = f32[4,2,2,32,256]{4,3,2,1,0:T(8,128)} collective-permute-done((f32[4,2,2,32,256]{4,3,2,1,0:T(8,128)S(1)}, f32[4,2,2,32,256]{4,3,2,1,0:T(8,128)}, u32[]{:S(2)}, u32[]{:S(2)}) %collective-permute-start.17) | collective-permute-done | bytes 524320 | tf_op jit(solution)/shard_map/ppermute | solution.py:24
  128.5 1.7 multiply_add_fusion.2
  135.7 7.8 %collective-permute-done.24 = f32[4,2,2,32,256]{4,3,2,1,0:T(8,128)S(1)} collective-permute-done((f32[4,2,2,32,256]{4,3,2,1,0:T(8,128)S(1)}, f32[4,2,2,32,256]{4,3,2,1,0:T(8,128)S(1)}, u32[]{:S(2)}, u32[]{:S(2)}) %collective-permute-start.24) | collective-permute-done | bytes 524320 | tf_op jit(solution)/shard_map/ppermute | solution.py:24
  145.3 1.3 multiply_subtract_fusion
  146.8 2.8 %collective-permute-start.26 = (f32[4,2,2,32,256]{4,3,2,1,0:T(8,128)S(1)}, f32[4,2,2,32,256]{4,3,2,1,0:T(8,128)S(1)}, u32[]{:S(2)}, u32[]{:S(2)}) collective-permute-start(f32[4,2,2,32,256]{4,3,2,1,0:T(8,128)S(1)} %multiply_add_fusion.refs_2_), channel_id=1, source_target_pairs={{0,1},{1,0},{2,3},{3,2},{4,5},{5,4},{6,7},{7,6},{8,9},{9,8},{10,11... | collective-permute-start | bytes 1572872 | tf_op jit(solution)/shard_map/ppermute | solution.py:24
  149.9 2.5 %collective-permute-start.33 = (f32[2,2,64,256]{3,2,1,0:T(8,128)S(1)}, f32[2,2,64,256]{3,2,1,0:T(8,128)S(1)}, u32[]{:S(2)}, u32[]{:S(2)}) collective-permute-start(f32[2,2,64,256]{3,2,1,0:T(8,128)S(1)} %copy-done.7), channel_id=1, source_target_pairs={{0,8},{4,12},{8,0},{12,4},{16,24},{20,28},{24,16},{28,20},{1,9},{5... | collective-permute-start | bytes 786440 | tf_op jit(solution)/shard_map/ppermute | solution.py:24
  154.2 8.0 %collective-permute-done.33.e1_ref = f32[2,2,64,256]{3,2,1,0:T(8,128)S(1)} collective-permute-done((f32[2,2,64,256]{3,2,1,0:T(8,128)S(1)}, f32[2,2,64,256]{3,2,1,0:T(8,128)S(1)}, u32[]{:S(2)}, u32[]{:S(2)}) %collective-permute-start.33) | collective-permute-done | bytes 262176 | tf_op jit(solution)/shard_map/ppermute | solution.py:24
  162.2 2.2 collective-permute-start.30
  166.9 3.3 %collective-permute-done.34.e2_ref = f32[2,2,64,256]{3,2,1,0:T(8,128)S(1)} collective-permute-done((f32[2,2,64,256]{3,2,1,0:T(8,128)S(1)}, f32[2,2,64,256]{3,2,1,0:T(8,128)S(1)}, u32[]{:S(2)}, u32[]{:S(2)}) %collective-permute-start.34) | collective-permute-done | bytes 262176 | tf_op jit(solution)/shard_map/ppermute | solution.py:24
  170.1 2.5 %collective-permute-start.27 = (f32[2,2,64,256]{3,2,1,0:T(8,128)S(1)}, f32[2,2,64,256]{3,2,1,0:T(8,128)S(1)}, u32[]{:S(2)}, u32[]{:S(2)}) collective-permute-start(f32[2,2,64,256]{3,2,1,0:T(8,128)S(1)} %get-tuple-element.150), channel_id=1, source_target_pairs={{0,8},{4,12},{8,0},{12,4},{16,24},{20,28},{24,16},{28,20},{1,9},{5... | collective-permute-start | bytes 786440 | tf_op jit(solution)/shard_map/ppermute | solution.py:24
  172.6 15.6 %collective-permute-done.35.e3_ref = f32[2,2,64,256]{3,2,1,0:T(8,128)S(1)} collective-permute-done((f32[2,2,64,256]{3,2,1,0:T(8,128)S(1)}, f32[2,2,64,256]{3,2,1,0:T(8,128)S(1)}, u32[]{:S(2)}, u32[]{:S(2)}) %collective-permute-start.35) | collective-permute-done | bytes 262176 | tf_op jit(solution)/shard_map/ppermute | solution.py:24
  188.2 1.4 collective-permute-start.29
  189.6 3.5 %finish.3.rest_0_ = f32[2,6,256,256]{3,2,1,0:T(8,128)} custom-call(bf16[2,512,512]{2,1,0:T(8,128)(2,1)S(1)} %pad_maximum_fusion.1.right_ref, bf16[2,512,512]{2,1,0:T(8,128)(2,1)S(1)} %pad_maximum_fusion.3.left_ref, f32[2,2,64,256]{3,2,1,0:T(8,128)S(1)} %get-tuple-element.111.e0_ref, f32[2,2,64,256]{3,2,1,0:T(8,128)S(1)} %collective-permute-done.33.e1_ref, ...), custom_call_target="tpu_custom_call" | custom-call | flops 1610612736 | bytes 2097152 | tf_op jit(solution)/shard_map/finish/pallas_call | solution.py:207
  193.1 10.9 %collective-permute-done.31.e2_ref = f32[2,2,64,256]{3,2,1,0:T(8,128)S(1)} collective-permute-done((f32[2,2,64,256]{3,2,1,0:T(8,128)S(1)}, f32[2,2,64,256]{3,2,1,0:T(8,128)S(1)}, u32[]{:S(2)}, u32[]{:S(2)}) %collective-permute-start.31) | collective-permute-done | bytes 262176 | tf_op jit(solution)/shard_map/ppermute | solution.py:24
  204.0 7.0 %collective-permute-done.32.e3_ref = f32[2,2,64,256]{3,2,1,0:T(8,128)S(1)} collective-permute-done((f32[2,2,64,256]{3,2,1,0:T(8,128)S(1)}, f32[2,2,64,256]{3,2,1,0:T(8,128)S(1)}, u32[]{:S(2)}, u32[]{:S(2)}) %collective-permute-start.32) | collective-permute-done | bytes 262176 | tf_op jit(solution)/shard_map/ppermute | solution.py:24
  211.0 3.5 %finish.4.rest_0_ = f32[2,6,256,256]{3,2,1,0:T(8,128)} custom-call(bf16[2,512,512]{2,1,0:T(8,128)(2,1)S(1)} %pad_maximum_fusion.1.right_ref, bf16[2,512,512]{2,1,0:T(8,128)(2,1)S(1)} %pad_maximum_fusion.3.left_ref, f32[2,2,64,256]{3,2,1,0:T(8,128)S(1)} %copy-done.1, ...), custom_call_target="tpu_custom_call", output_to_operand_aliasing={{}: (6, {})} | custom-call | flops 1610612736 | bytes 2097152 | tf_op jit(solution)/shard_map/finish/pallas_call | solution.py:207
  215.4 6.9 %collective-permute-done.29.e3_ref = f32[2,2,64,256]{3,2,1,0:T(8,128)S(1)} collective-permute-done((f32[2,2,64,256]{3,2,1,0:T(8,128)S(1)}, f32[2,2,64,256]{3,2,1,0:T(8,128)S(1)}, u32[]{:S(2)}, u32[]{:S(2)}) %collective-permute-start.29) | collective-permute-done | bytes 262176 | tf_op jit(solution)/shard_map/ppermute | solution.py:24
  222.3 3.5 %finish.5 = f32[2,6,256,256]{3,2,1,0:T(8,128)} custom-call(bf16[2,512,512]{2,1,0:T(8,128)(2,1)S(1)} %pad_maximum_fusion.1.right_ref, bf16[2,512,512]{2,1,0:T(8,128)(2,1)S(1)} %pad_maximum_fusion.3.left_ref, f32[2,2,64,256]{3,2,1,0:T(8,128)S(1)} %get-tuple-element.149.e0_ref, ...), custom_call_target="tpu_custom_call", output_to_operand_aliasing={{}: (6, {})} | custom-call | flops 1610612736 | bytes 2097152 | tf_op jit(solution)/shard_map/finish/pallas_call | solution.py:207
  (120 shorter events, 41.2 us)
Async XLA Ops:
  1.3 18.5 %collective-permute-start.8 = (f32[2,2,64,256]{3,2,1,0:T(8,128)S(1)}, f32[2,2,64,256]{3,2,1,0:T(8,128)S(1)}, u32[]{:S(2)}, u32[]{:S(2)}) collective-permute-start(f32[2,2,64,256]{3,2,1,0:T(8,128)S(1)} %get-tuple-element.161), channel_id=1, source_target_pairs={{0,24},{4,28},{8,16},{12,20},{16,8},{20,12},{24,0},{28,4},{1,25},{... | collective-permute-start | bytes 786440 | tf_op jit(solution)/shard_map/ppermute | solution.py:24
  1.5 22.0 %collective-permute-start.7 = (f32[2,2,64,256]{3,2,1,0:T(8,128)S(1)}, f32[2,2,64,256]{3,2,1,0:T(8,128)S(1)}, u32[]{:S(2)}, u32[]{:S(2)}) collective-permute-start(f32[2,2,64,256]{3,2,1,0:T(8,128)S(1)} %get-tuple-element.162), channel_id=1, source_target_pairs={{0,16},{4,20},{8,24},{12,28},{16,0},{20,4},{24,8},{28,12},{1,17},{... | collective-permute-start | bytes 786440 | tf_op jit(solution)/shard_map/ppermute | solution.py:24
  4.7 18.8 %collective-permute-start.6 = (f32[2,2,64,256]{3,2,1,0:T(8,128)S(1)}, f32[2,2,64,256]{3,2,1,0:T(8,128)S(1)}, u32[]{:S(2)}, u32[]{:S(2)}) collective-permute-start(f32[2,2,64,256]{3,2,1,0:T(8,128)S(1)} %get-tuple-element.163), channel_id=1, source_target_pairs={{0,8},{4,12},{8,0},{12,4},{16,24},{20,28},{24,16},{28,20},{1,9},{5... | collective-permute-start | bytes 786440 | tf_op jit(solution)/shard_map/ppermute | solution.py:24
  24.7 12.2 %collective-permute-start.9 = (f32[4,2,2,32,256]{4,3,2,1,0:T(8,128)S(1)}, f32[4,2,2,32,256]{4,3,2,1,0:T(8,128)S(1)}, u32[]{:S(2)}, u32[]{:S(2)}) collective-permute-start(f32[4,2,2,32,256]{4,3,2,1,0:T(8,128)S(1)} %get-tuple-element.93), channel_id=1, source_target_pairs={{0,4},{4,0},{8,12},{12,8},{16,20},{20,16},{24,28},{28,24},{1,5},{5... | collective-permute-start | bytes 1572872 | tf_op jit(solution)/shard_map/ppermute | solution.py:24
  26.0 11.9 %collective-permute-start.10 = (f32[4,2,2,32,256]{4,3,2,1,0:T(8,128)S(1)}, f32[4,2,2,32,256]{4,3,2,1,0:T(8,128)S(1)}, u32[]{:S(2)}, u32[]{:S(2)}) collective-permute-start(f32[4,2,2,32,256]{4,3,2,1,0:T(8,128)S(1)} %get-tuple-element.95), channel_id=1, source_target_pairs={{0,2},{1,3},{2,0},{3,1},{4,6},{5,7},{6,4},{7,5},{8,10},{9,11},{10,... | collective-permute-start | bytes 1572872 | tf_op jit(solution)/shard_map/ppermute | solution.py:24
  39.8 23.5 %collective-permute-start.14 = (f32[4,2,2,32,256]{4,3,2,1,0:T(8,128)S(1)}, f32[4,2,2,32,256]{4,3,2,1,0:T(8,128)S(1)}, u32[]{:S(2)}, u32[]{:S(2)}) collective-permute-start(f32[4,2,2,32,256]{4,3,2,1,0:T(8,128)S(1)} %pad_maximum_fusion.4), channel_id=1, source_target_pairs={{0,4},{4,0},{8,12},{12,8},{16,20},{20,16},{24,28},{28,24},{1,5},{5... | collective-permute-start | bytes 1572872 | tf_op jit(solution)/shard_map/ppermute | solution.py:24
  40.3 23.0 %collective-permute-start.13 = (f32[4,2,2,32,256]{4,3,2,1,0:T(8,128)S(1)}, f32[4,2,2,32,256]{4,3,2,1,0:T(8,128)S(1)}, u32[]{:S(2)}, u32[]{:S(2)}) collective-permute-start(f32[4,2,2,32,256]{4,3,2,1,0:T(8,128)S(1)} %multiply_add_fusion.11), channel_id=1, source_target_pairs={{0,2},{1,3},{2,0},{3,1},{4,6},{5,7},{6,4},{7,5},{8,10},{9,11},{10,... | collective-permute-start | bytes 1572872 | tf_op jit(solution)/shard_map/ppermute | solution.py:24
  41.7 20.5 %collective-permute-start.4 = (f32[2,2,64,256]{3,2,1,0:T(8,128)S(1)}, f32[2,2,64,256]{3,2,1,0:T(8,128)S(1)}, u32[]{:S(2)}, u32[]{:S(2)}) collective-permute-start(f32[2,2,64,256]{3,2,1,0:T(8,128)S(1)} %get-tuple-element.158), channel_id=1, source_target_pairs={{0,16},{4,20},{8,24},{12,28},{16,0},{20,4},{24,8},{28,12},{1,17},{... | collective-permute-start | bytes 786440 | tf_op jit(solution)/shard_map/ppermute | solution.py:24
  45.7 16.5 %collective-permute-start.3 = (f32[2,2,64,256]{3,2,1,0:T(8,128)S(1)}, f32[2,2,64,256]{3,2,1,0:T(8,128)S(1)}, u32[]{:S(2)}, u32[]{:S(2)}) collective-permute-start(f32[2,2,64,256]{3,2,1,0:T(8,128)S(1)} %get-tuple-element.159), channel_id=1, source_target_pairs={{0,8},{4,12},{8,0},{12,4},{16,24},{20,28},{24,16},{28,20},{1,9},{5... | collective-permute-start | bytes 786440 | tf_op jit(solution)/shard_map/ppermute | solution.py:24
  65.4 6.5 %collective-permute-start.16 = (f32[4,2,2,32,256]{4,3,2,1,0:T(8,128)S(1)}, f32[4,2,2,32,256]{4,3,2,1,0:T(8,128)S(1)}, u32[]{:S(2)}, u32[]{:S(2)}) collective-permute-start(f32[4,2,2,32,256]{4,3,2,1,0:T(8,128)S(1)} %multiply_add_fusion.8.refs_2_), channel_id=1, source_target_pairs={{0,1},{1,0},{2,3},{3,2},{4,5},{5,4},{6,7},{7,6},{8,9},{9,8},{10,11... | collective-permute-start | bytes 1572872 | tf_op jit(solution)/shard_map/ppermute | solution.py:24
  68.7 13.1 %collective-permute-start.11 = (f32[4,2,2,32,256]{4,3,2,1,0:T(8,128)S(1)}, f32[4,2,2,32,256]{4,3,2,1,0:T(8,128)S(1)}, u32[]{:S(2)}, u32[]{:S(2)}) collective-permute-start(f32[4,2,2,32,256]{4,3,2,1,0:T(8,128)S(1)} %get-tuple-element.115), channel_id=1, source_target_pairs={{0,4},{4,0},{8,12},{12,8},{16,20},{20,16},{24,28},{28,24},{1,5},{5... | collective-permute-start | bytes 1572872 | tf_op jit(solution)/shard_map/ppermute | solution.py:24
  70.0 12.8 %collective-permute-start.12 = (f32[4,2,2,32,256]{4,3,2,1,0:T(8,128)S(1)}, f32[4,2,2,32,256]{4,3,2,1,0:T(8,128)S(1)}, u32[]{:S(2)}, u32[]{:S(2)}) collective-permute-start(f32[4,2,2,32,256]{4,3,2,1,0:T(8,128)S(1)} %get-tuple-element.117), channel_id=1, source_target_pairs={{0,2},{1,3},{2,0},{3,1},{4,6},{5,7},{6,4},{7,5},{8,10},{9,11},{10,... | collective-permute-start | bytes 1572872 | tf_op jit(solution)/shard_map/ppermute | solution.py:24
  84.7 24.6 %collective-permute-start.20 = (f32[4,2,2,32,256]{4,3,2,1,0:T(8,128)S(1)}, f32[4,2,2,32,256]{4,3,2,1,0:T(8,128)S(1)}, u32[]{:S(2)}, u32[]{:S(2)}) collective-permute-start(f32[4,2,2,32,256]{4,3,2,1,0:T(8,128)S(1)} %pad_maximum_fusion.6), channel_id=1, source_target_pairs={{0,4},{4,0},{8,12},{12,8},{16,20},{20,16},{24,28},{28,24},{1,5},{5... | collective-permute-start | bytes 1572872 | tf_op jit(solution)/shard_map/ppermute | solution.py:24
  85.2 24.1 %collective-permute-start.19 = (f32[4,2,2,32,256]{4,3,2,1,0:T(8,128)S(1)}, f32[4,2,2,32,256]{4,3,2,1,0:T(8,128)S(1)}, u32[]{:S(2)}, u32[]{:S(2)}) collective-permute-start(f32[4,2,2,32,256]{4,3,2,1,0:T(8,128)S(1)} %multiply_add_fusion.7), channel_id=1, source_target_pairs={{0,2},{1,3},{2,0},{3,1},{4,6},{5,7},{6,4},{7,5},{8,10},{9,11},{10,... | collective-permute-start | bytes 1572872 | tf_op jit(solution)/shard_map/ppermute | solution.py:24
  86.6 5.8 %collective-permute-start.2 = (f32[2,2,64,256]{3,2,1,0:T(8,128)S(1)}, f32[2,2,64,256]{3,2,1,0:T(8,128)S(1)}, u32[]{:S(2)}, u32[]{:S(2)}) collective-permute-start(f32[2,2,64,256]{3,2,1,0:T(8,128)S(1)} %get-tuple-element.153), channel_id=1, source_target_pairs={{0,24},{4,28},{8,16},{12,20},{16,8},{20,12},{24,0},{28,4},{1,25},{... | collective-permute-start | bytes 786440 | tf_op jit(solution)/shard_map/ppermute | solution.py:24
  87.6 20.5 %collective-permute-start.1 = (f32[2,2,64,256]{3,2,1,0:T(8,128)S(1)}, f32[2,2,64,256]{3,2,1,0:T(8,128)S(1)}, u32[]{:S(2)}, u32[]{:S(2)}) collective-permute-start(f32[2,2,64,256]{3,2,1,0:T(8,128)S(1)} %get-tuple-element.154), channel_id=1, source_target_pairs={{0,16},{4,20},{8,24},{12,28},{16,0},{20,4},{24,8},{28,12},{1,17},{... | collective-permute-start | bytes 786440 | tf_op jit(solution)/shard_map/ppermute | solution.py:24
  91.6 16.6 %collective-permute-start = (f32[2,2,64,256]{3,2,1,0:T(8,128)S(1)}, f32[2,2,64,256]{3,2,1,0:T(8,128)S(1)}, u32[]{:S(2)}, u32[]{:S(2)}) collective-permute-start(f32[2,2,64,256]{3,2,1,0:T(8,128)S(1)} %get-tuple-element.155), channel_id=1, source_target_pairs={{0,8},{4,12},{8,0},{12,4},{16,24},{20,28},{24,16},{28,20},{1,9},{5... | collective-permute-start | bytes 786440 | tf_op jit(solution)/shard_map/ppermute | solution.py:24
  114.4 13.2 %collective-permute-start.17 = (f32[4,2,2,32,256]{4,3,2,1,0:T(8,128)S(1)}, f32[4,2,2,32,256]{4,3,2,1,0:T(8,128)}, u32[]{:S(2)}, u32[]{:S(2)}) collective-permute-start(f32[4,2,2,32,256]{4,3,2,1,0:T(8,128)S(1)} %get-tuple-element.137), channel_id=1, source_target_pairs={{0,4},{4,0},{8,12},{12,8},{16,20},{20,16},{24,28},{28,24},{1,5},{5... | collective-permute-start | bytes 1572872 | tf_op jit(solution)/shard_map/ppermute | solution.py:24
  115.6 12.9 %collective-permute-start.18 = (f32[4,2,2,32,256]{4,3,2,1,0:T(8,128)S(1)}, f32[4,2,2,32,256]{4,3,2,1,0:T(8,128)}, u32[]{:S(2)}, u32[]{:S(2)}) collective-permute-start(f32[4,2,2,32,256]{4,3,2,1,0:T(8,128)S(1)} %get-tuple-element.139), channel_id=1, source_target_pairs={{0,2},{1,3},{2,0},{3,1},{4,6},{5,7},{6,4},{7,5},{8,10},{9,11},{10,... | collective-permute-start | bytes 1572872 | tf_op jit(solution)/shard_map/ppermute | solution.py:24
  131.5 12.0 %collective-permute-start.24 = (f32[4,2,2,32,256]{4,3,2,1,0:T(8,128)S(1)}, f32[4,2,2,32,256]{4,3,2,1,0:T(8,128)S(1)}, u32[]{:S(2)}, u32[]{:S(2)}) collective-permute-start(f32[4,2,2,32,256]{4,3,2,1,0:T(8,128)S(1)} %pad_maximum_fusion.8), channel_id=1, source_target_pairs={{0,4},{4,0},{8,12},{12,8},{16,20},{20,16},{24,28},{28,24},{1,5},{5... | collective-permute-start | bytes 1572872 | tf_op jit(solution)/shard_map/ppermute | solution.py:24
  133.0 11.7 %collective-permute-start.23 = (f32[4,2,2,32,256]{4,3,2,1,0:T(8,128)S(1)}, f32[4,2,2,32,256]{4,3,2,1,0:T(8,128)S(1)}, u32[]{:S(2)}, u32[]{:S(2)}) collective-permute-start(f32[4,2,2,32,256]{4,3,2,1,0:T(8,128)S(1)} %multiply_add_fusion.3), channel_id=1, source_target_pairs={{0,2},{1,3},{2,0},{3,1},{4,6},{5,7},{6,4},{7,5},{8,10},{9,11},{10,... | collective-permute-start | bytes 1572872 | tf_op jit(solution)/shard_map/ppermute | solution.py:24
  146.8 17.8 %collective-permute-start.26 = (f32[4,2,2,32,256]{4,3,2,1,0:T(8,128)S(1)}, f32[4,2,2,32,256]{4,3,2,1,0:T(8,128)S(1)}, u32[]{:S(2)}, u32[]{:S(2)}) collective-permute-start(f32[4,2,2,32,256]{4,3,2,1,0:T(8,128)S(1)} %multiply_add_fusion.refs_2_), channel_id=1, source_target_pairs={{0,1},{1,0},{2,3},{3,2},{4,5},{5,4},{6,7},{7,6},{8,9},{9,8},{10,11... | collective-permute-start | bytes 1572872 | tf_op jit(solution)/shard_map/ppermute | solution.py:24
  149.6 15.2 %collective-permute-start.25 = (f32[4,2,2,32,256]{4,3,2,1,0:T(8,128)S(1)}, f32[4,2,2,32,256]{4,3,2,1,0:T(8,128)S(1)}, u32[]{:S(2)}, u32[]{:S(2)}) collective-permute-start(f32[4,2,2,32,256]{4,3,2,1,0:T(8,128)S(1)} %pad_maximum_fusion.9.refs_0_), channel_id=1, source_target_pairs={{0,1},{1,0},{2,3},{3,2},{4,5},{5,4},{6,7},{7,6},{8,9},{9,8},{10,11... | collective-permute-start | bytes 1572872 | tf_op jit(solution)/shard_map/ppermute | solution.py:24
  149.9 12.3 %collective-permute-start.33 = (f32[2,2,64,256]{3,2,1,0:T(8,128)S(1)}, f32[2,2,64,256]{3,2,1,0:T(8,128)S(1)}, u32[]{:S(2)}, u32[]{:S(2)}) collective-permute-start(f32[2,2,64,256]{3,2,1,0:T(8,128)S(1)} %copy-done.7), channel_id=1, source_target_pairs={{0,8},{4,12},{8,0},{12,4},{16,24},{20,28},{24,16},{28,20},{1,9},{5... | collective-permute-start | bytes 786440 | tf_op jit(solution)/shard_map/ppermute | solution.py:24
  152.6 17.5 %collective-permute-start.34 = (f32[2,2,64,256]{3,2,1,0:T(8,128)S(1)}, f32[2,2,64,256]{3,2,1,0:T(8,128)S(1)}, u32[]{:S(2)}, u32[]{:S(2)}) collective-permute-start(f32[2,2,64,256]{3,2,1,0:T(8,128)S(1)} %copy-done.5), channel_id=1, source_target_pairs={{0,16},{4,20},{8,24},{12,28},{16,0},{20,4},{24,8},{28,12},{1,17},{... | collective-permute-start | bytes 786440 | tf_op jit(solution)/shard_map/ppermute | solution.py:24
  153.7 34.6 %collective-permute-start.35 = (f32[2,2,64,256]{3,2,1,0:T(8,128)S(1)}, f32[2,2,64,256]{3,2,1,0:T(8,128)S(1)}, u32[]{:S(2)}, u32[]{:S(2)}) collective-permute-start(f32[2,2,64,256]{3,2,1,0:T(8,128)S(1)} %copy-done.3), channel_id=1, source_target_pairs={{0,24},{4,28},{8,16},{12,20},{16,8},{20,12},{24,0},{28,4},{1,25},{... | collective-permute-start | bytes 786440 | tf_op jit(solution)/shard_map/ppermute | solution.py:24
  162.2 26.0 %collective-permute-start.30 = (f32[2,2,64,256]{3,2,1,0:T(8,128)S(1)}, f32[2,2,64,256]{3,2,1,0:T(8,128)S(1)}, u32[]{:S(2)}, u32[]{:S(2)}) collective-permute-start(f32[2,2,64,256]{3,2,1,0:T(8,128)S(1)} %copy-done.13), channel_id=1, source_target_pairs={{0,8},{4,12},{8,0},{12,4},{16,24},{20,28},{24,16},{28,20},{1,9},{5... | collective-permute-start | bytes 786440 | tf_op jit(solution)/shard_map/ppermute | solution.py:24
  164.6 39.5 %collective-permute-start.31 = (f32[2,2,64,256]{3,2,1,0:T(8,128)S(1)}, f32[2,2,64,256]{3,2,1,0:T(8,128)S(1)}, u32[]{:S(2)}, u32[]{:S(2)}) collective-permute-start(f32[2,2,64,256]{3,2,1,0:T(8,128)S(1)} %copy-done.11), channel_id=1, source_target_pairs={{0,16},{4,20},{8,24},{12,28},{16,0},{20,4},{24,8},{28,12},{1,17},{... | collective-permute-start | bytes 786440 | tf_op jit(solution)/shard_map/ppermute | solution.py:24
  164.9 46.2 %collective-permute-start.32 = (f32[2,2,64,256]{3,2,1,0:T(8,128)S(1)}, f32[2,2,64,256]{3,2,1,0:T(8,128)S(1)}, u32[]{:S(2)}, u32[]{:S(2)}) collective-permute-start(f32[2,2,64,256]{3,2,1,0:T(8,128)S(1)} %copy-done.9), channel_id=1, source_target_pairs={{0,24},{4,28},{8,16},{12,20},{16,8},{20,12},{24,0},{28,4},{1,25},{... | collective-permute-start | bytes 786440 | tf_op jit(solution)/shard_map/ppermute | solution.py:24
  170.1 44.4 %collective-permute-start.27 = (f32[2,2,64,256]{3,2,1,0:T(8,128)S(1)}, f32[2,2,64,256]{3,2,1,0:T(8,128)S(1)}, u32[]{:S(2)}, u32[]{:S(2)}) collective-permute-start(f32[2,2,64,256]{3,2,1,0:T(8,128)S(1)} %get-tuple-element.150), channel_id=1, source_target_pairs={{0,8},{4,12},{8,0},{12,4},{16,24},{20,28},{24,16},{28,20},{1,9},{5... | collective-permute-start | bytes 786440 | tf_op jit(solution)/shard_map/ppermute | solution.py:24
  188.2 27.2 %collective-permute-start.28 = (f32[2,2,64,256]{3,2,1,0:T(8,128)S(1)}, f32[2,2,64,256]{3,2,1,0:T(8,128)S(1)}, u32[]{:S(2)}, u32[]{:S(2)}) collective-permute-start(f32[2,2,64,256]{3,2,1,0:T(8,128)S(1)} %get-tuple-element.151), channel_id=1, source_target_pairs={{0,16},{4,20},{8,24},{12,28},{16,0},{20,4},{24,8},{28,12},{1,17},{... | collective-permute-start | bytes 786440 | tf_op jit(solution)/shard_map/ppermute | solution.py:24
  188.2 34.0 %collective-permute-start.29 = (f32[2,2,64,256]{3,2,1,0:T(8,128)S(1)}, f32[2,2,64,256]{3,2,1,0:T(8,128)S(1)}, u32[]{:S(2)}, u32[]{:S(2)}) collective-permute-start(f32[2,2,64,256]{3,2,1,0:T(8,128)S(1)} %get-tuple-element.152), channel_id=1, source_target_pairs={{0,24},{4,28},{8,16},{12,20},{16,8},{20,12},{24,0},{28,4},{1,25},{... | collective-permute-start | bytes 786440 | tf_op jit(solution)/shard_map/ppermute | solution.py:24
  (19 other events, 214.6 us)
where the time goes:
time: 228 us; the launch traced here: 226 us
  waiting for transfers between devices  145 us (64%)
  starting transfers between devices  42.5 us (19%)
  other arithmetic  17.2 us (8%)
  Pallas kernels  16.6 us (7%)
  local copies, waits for them, and re-layouts  4.15 us (2%)
    ppermute x36, waiting for transfers between devices, exchanged(): return lax.ppermute(block, axis, [(i, i ^ mask) for i in range(count)])  145 us
    ppermute x36, starting transfers between devices, exchanged(): return lax.ppermute(block, axis, [(i, i ^ mask) for i in range(count)])  42.5 us
    pallas_call x3, Pallas kernels, finish(): pl.pallas_call(functools.partial(finish_kernel, start), in_specs=in_specs...  10.6 us
    sub x6, other arithmetic, turned(): real * cosine - imag * sine  7.66 us
    add x12, other arithmetic, butterfly(): both = own * pair[0] + other  6.45 us
  transfers between devices with their start and end apart: 36, of which 22 were waited for; matrix products, arithmetic and copies ran while one was open for 3% of the time, Pallas kernels for 5%

commit v1 on v0

--- a/solution.py
+++ b/solution.py
@@ -89,16 +89,6 @@
 
 def after(value, done):
     return value if done is None else lax.optimization_barrier((value, done))[0]
-
-
-def turned(values, cosine, sine):
-    real, imag = values[:, :1], values[:, 1:]
-    return jnp.concatenate([real * cosine - imag * sine, real * sine + imag * cosine], axis=1)
-
-
-def butterfly(own, other, pair, bit):
-    both = own * pair[0] + other
-    return turned(both, pair[1], pair[2]) if bit else both
 
 
 def per_rows(planes, rows, step, body):
@@ -145,36 +135,47 @@
     )(coefs, *pieces)
 
 
-def join_kernel(twist, coef_ref, *refs):
-    sides, outs = (refs[0:2], refs[2:4]), refs[4:]
-    groups, _, planes, half, _ = refs[0].shape
-    flip = coef_ref[0]
-    for h, (own_ref, other_ref) in enumerate(sides):
-
-        def body(plane, at, h=h, own_ref=own_ref, other_ref=other_ref):
-            rows, into = pl.ds(at, 8), pl.ds(h * half + at, 8)
+def butterfly_kernel(kinds, apart, *refs):
+    sides, outs = refs[2:6], refs[6:]
+    groups, _, planes, half, _ = sides[0].shape
+    for h, (source, at_coef, twist) in enumerate(kinds):
+        coef_ref, own_ref, other_ref = refs[source], sides[2 * h], sides[2 * h + 1]
+        flip, c, s = [coef_ref[at_coef + i] for i in range(3)]
+
+        def body(plane, at):
+            rows = pl.ds(at, 8)
             for e in range(groups):
                 real, imag = [own_ref[e, p, plane, rows, :] * flip + other_ref[e, p, plane, rows, :] for p in range(2)]
                 if twist:
-                    real, imag = real * coef_ref[1] - imag * coef_ref[2], real * coef_ref[2] + imag * coef_ref[1]
-                outs[e][0, plane, into, :] = real
-                outs[e][1, plane, into, :] = imag
+                    real, imag = real * c - imag * s, real * s + imag * c
+                if apart:
+                    into = pl.ds(h * half + at, 8)
+                    outs[e][0, plane, into, :] = real
+                    outs[e][1, plane, into, :] = imag
+                else:
+                    outs[h][e, 0, plane, rows, :] = real
+                    outs[h][e, 1, plane, rows, :] = imag
 
         per_rows(planes, half, 8, body)
 
 
-def join(own, other, pair, bit):
+def butterfly(own, other, kinds, coefs, apart):
     groups, _, planes, half, columns = own[0].shape
-    piece = jax.ShapeDtypeStruct((2, planes, 2 * half, columns), F32)
-    return pl.pallas_call(
-        functools.partial(join_kernel, bit > 0),
-        in_specs=[SMEM] + [VMEM] * 4,
-        out_specs=[VMEM] * groups,
-        out_shape=[piece] * groups,
-        compiler_params=pltpu.CompilerParams(vmem_limit_bytes=GRANT),
-        cost_estimate=estimate(10 * own[0].size, 6 * own[0].size),
-        name="join",
-    )(pair, own[0], other[0], own[1], other[1])
+    if apart:
+        shapes = [jax.ShapeDtypeStruct((2, planes, 2 * half, columns), F32)] * groups
+    else:
+        shapes = [jax.ShapeDtypeStruct(own[0].shape, F32)] * 2
+    return list(
+        pl.pallas_call(
+            functools.partial(butterfly_kernel, kinds, apart),
+            in_specs=[SMEM] * 2 + [VMEM] * 4,
+            out_specs=[VMEM] * len(shapes),
+            out_shape=shapes,
+            compiler_params=pltpu.CompilerParams(vmem_limit_bytes=GRANT),
+            cost_estimate=estimate(10 * own[0].size, 6 * own[0].size),
+            name="butterfly",
+        )(*coefs, own[0], other[0], own[1], other[1])
+    )
 
 
 def finish_kernel(start, right_ref, left_ref, e0_ref, e1_ref, e2_ref, e3_ref, *rest):
@@ -247,15 +248,20 @@
 
 
 def chunks_of(planes):
-    size = max(1, planes // 3)
-    starts = list(range(0, planes, size))
-    return [(at, min(size, planes - at)) for at in starts]
+    edge = max(1, planes // 6)
+    middle = max(1, (planes - 2 * edge + 1) // 2)
+    starts, chunks = 0, []
+    for size in (edge, middle, planes - 2 * edge - middle, edge):
+        size = min(size, planes - starts)
+        if size > 0:
+            chunks.append((starts, size))
+            starts += size
+    return chunks
 
 
 def order_of(chunks, steps):
-    sizes = [size / chunks[0][1] for _, size in chunks]
     ready, at, free, order = [], 0.5, 0.0, []
-    for i, size in enumerate(sizes):
+    for i, (_, size) in enumerate(chunks):
         at += size
         ready.append((at, i, 0))
     while ready:
@@ -263,10 +269,10 @@
         now, i, step = ready.pop(0)
         order.append((i, step))
         if step < steps - 2:
-            free = max(now + 0.1, free) + sizes[i] / 2
+            free = max(now + 0.2, free) + chunks[i][1] / 2
             ready.append((free, i, step + 1))
         elif step < steps - 1:
-            ready.append((now + 0.1, i, step + 1))
+            ready.append((now + 0.3, i, step + 1))
     return order
 
 
@@ -298,11 +304,14 @@
         quarters = after(quarters, pieces)
         received.append(pieces[:1] + [exchanged(pieces[d], "gz", d * stride) for d in range(1, 4)])
 
-    coefs = row_of(mix_table(z_count), z_index)
+    z_steps, y_steps = list(reversed(range(z_bits - 2))), list(reversed(range(y_bits)))
+    z_table = np.concatenate([mix_table(z_count)] + [pair_table(z_count, bit) for bit in z_steps], axis=1)
+    y_table = np.concatenate([pair_table(y_count, bit) for bit in y_steps], axis=1)
+    coefs = [row_of(z_table, z_index), row_of(y_table, y_index)]
     right = right_matrix(shifts[0].astype(jnp.int32), z_count, columns)
     left = left_matrix(shifts[1].astype(jnp.int32), y_count, rows, part.astype(jnp.int32))
-    z_pairs = [("gz", bit, row_of(pair_table(z_count, bit), z_index)) for bit in reversed(range(z_bits - 2))]
-    y_pairs = [("gy", bit, row_of(pair_table(y_count, bit), y_index)) for bit in reversed(range(y_bits))]
+    z_pairs = [("gz", bit, (0, 32 + 3 * i, bit > 0)) for i, bit in enumerate(z_steps)]
+    y_pairs = [("gy", bit, (1, 3 * i, bit > 0)) for i, bit in enumerate(y_steps)]
     ways = list(zip(z_pairs + y_pairs[:-1], y_pairs[:-1] + z_pairs))
     ways.append((y_pairs[-1], y_pairs[-1]))
 
@@ -313,15 +322,12 @@
     for i, step in order_of(chunks, steps):
         if step == 0:
             pieces = after(received[i], done)
-            state[i] = mix(pieces, coefs)
+            state[i] = mix(pieces, coefs[0])
         else:
             way = ways[step - 1]
             other = [exchanged(block, axis, 2**bit) for block, (axis, bit, _) in zip(state[i], way)]
             own, other = after((state[i], other), done)
-            if step == steps - 1:
-                pieces = list(join(own, other, way[0][2], way[0][1]))
-            else:
-                pieces = [butterfly(a, b, pair, bit) for a, b, (_, bit, pair) in zip(own, other, way)]
+            pieces = butterfly(own, other, tuple(pair for _, _, pair in way), coefs, step == steps - 1)
             state[i] = pieces
             if step == steps - 1:
                 back[i] = pieces[:1] + [exchanged(pieces[d], "gz", d * stride) for d in range(1, 4)]

time: 228 us -> 223 us (0.978)
  waiting for transfers between devices: 145 us -> 125 us
  starting transfers between devices: 42.5 us -> 57.9 us
  other arithmetic: 17.2 us -> 2.92 us
  Pallas kernels: 16.6 us -> 23.8 us
  local copies, waits for them, and re-layouts: 4.15 us -> 8.35 us
    ppermute x36 -> x48, waiting for transfers between devices: 145 us -> 125 us  [exchanged(): return lax.ppermute(block, axis, [(i, i ^ mask) for i in range(count)])]
    ppermute x36 -> x48, starting transfers between devices: 42.5 us -> 57.9 us  [exchanged(): return lax.ppermute(block, axis, [(i, i ^ mask) for i in range(count)])]
    sub x6 -> x0, other arithmetic: 7.66 us -> none  [turned(): real * cosine - imag * sine]
    add x12 -> x0, other arithmetic: 6.45 us -> none  [butterfly(): both = own * pair[0] + other]
    pallas_call x3 -> x12, Pallas kernels: 2.43 us -> 8.52 us  [butterfly(): pl.pallas_call(functools.partial(butterfly_kernel, kinds, apart), in_spec...]
    unnamed x30 -> x22, local copies, waits for them, and re-layouts: 0.07 us -> 3.7 us
    pallas_call x3 -> x4, Pallas kernels: 10.6 us -> 10.9 us  [finish(): pl.pallas_call(functools.partial(finish_kernel, start), in_specs=in_specs...]
  transfers between devices with their start and end apart: 36 -> 48, of which waited for: 22 -> 18; matrix products, arithmetic and copies ran while one was open for 3% -> 3% of each run, Pallas kernels for 5% -> 7%
where the time goes in v1:
time: 223 us; the launch traced here: 219 us
  waiting for transfers between devices  125 us (56%)
  starting transfers between devices  57.9 us (26%)
  Pallas kernels  23.8 us (11%)
  local copies, waits for them, and re-layouts  8.35 us (4%)
  other arithmetic  2.92 us (1%)
    ppermute x48, waiting for transfers between devices, exchanged(): return lax.ppermute(block, axis, [(i, i ^ mask) for i in range(count)])  125 us
    ppermute x48, starting transfers between devices, exchanged(): return lax.ppermute(block, axis, [(i, i ^ mask) for i in range(count)])  57.9 us
    pallas_call x4, Pallas kernels, finish(): pl.pallas_call(functools.partial(finish_kernel, start), in_specs=in_specs...  10.9 us
    pallas_call x12, Pallas kernels, butterfly(): pl.pallas_call(functools.partial(butterfly_kernel, kinds, apart), in_spec...  8.52 us
  transfers between devices with their start and end apart: 48, of which 18 were waited for; matrix products, arithmetic and copies ran while one was open for 3% of the time, Pallas kernels for 7%

profile of v1, /device:TPU:19, one launch (start us, length us, event | category | flops | bytes accessed | tf_op | source)
XLA Modules:
  0.0 218.8 jit_solution(16604869745699208914)
XLA Ops:
  1.5 3.2 %collective-permute-start.7 = (f32[2,1,64,256]{3,2,1,0:T(8,128)S(1)}, f32[2,1,64,256]{3,2,1,0:T(8,128)S(1)}, u32[]{:S(2)}, u32[]{:S(2)}) collective-permute-start(f32[2,1,64,256]{3,2,1,0:T(8,128)S(1)} %get-tuple-element.244), channel_id=1, source_target_pairs={{0,16},{4,20},{8,24},{12,28},{16,0},{20,4},{24,8},{28,12},{1,17},{... | collective-permute-start | bytes 393224 | tf_op jit(solution)/shard_map/ppermute | solution.py:24
  5.4 3.5 %collective-permute-done.8.refs_3_ = f32[2,1,64,256]{3,2,1,0:T(8,128)S(1)} collective-permute-done((f32[2,1,64,256]{3,2,1,0:T(8,128)S(1)}, f32[2,1,64,256]{3,2,1,0:T(8,128)S(1)}, u32[]{:S(2)}, u32[]{:S(2)}) %collective-permute-start.8) | collective-permute-done | bytes 131104 | tf_op jit(solution)/shard_map/ppermute | solution.py:24
  8.9 3.4 %collective-permute-done.7.refs_2_ = f32[2,1,64,256]{3,2,1,0:T(8,128)S(1)} collective-permute-done((f32[2,1,64,256]{3,2,1,0:T(8,128)S(1)}, f32[2,1,64,256]{3,2,1,0:T(8,128)S(1)}, u32[]{:S(2)}, u32[]{:S(2)}) %collective-permute-start.7) | collective-permute-done | bytes 131104 | tf_op jit(solution)/shard_map/ppermute | solution.py:24
  15.4 4.0 %collective-permute-done.9.refs_3_ = f32[4,2,1,32,256]{4,3,2,1,0:T(8,128)S(1)} collective-permute-done((f32[4,2,1,32,256]{4,3,2,1,0:T(8,128)S(1)}, f32[4,2,1,32,256]{4,3,2,1,0:T(8,128)S(1)}, u32[]{:S(2)}, u32[]{:S(2)}) %collective-permute-start.9) | collective-permute-done | bytes 262176 | tf_op jit(solution)/shard_map/ppermute | solution.py:24
  21.6 4.7 %collective-permute-done.11.refs_3_ = f32[4,2,1,32,256]{4,3,2,1,0:T(8,128)S(1)} collective-permute-done((f32[4,2,1,32,256]{4,3,2,1,0:T(8,128)S(1)}, f32[4,2,1,32,256]{4,3,2,1,0:T(8,128)S(1)}, u32[]{:S(2)}, u32[]{:S(2)}) %collective-permute-start.11) | collective-permute-done | bytes 262176 | tf_op jit(solution)/shard_map/ppermute | solution.py:24
  27.1 4.3 %collective-permute-start.13 = (f32[4,2,1,32,256]{4,3,2,1,0:T(8,128)S(1)}, f32[4,2,1,32,256]{4,3,2,1,0:T(8,128)S(1)}, u32[]{:S(2)}, u32[]{:S(2)}) collective-permute-start(f32[4,2,1,32,256]{4,3,2,1,0:T(8,128)S(1)} %get-tuple-element.145.refs_2_), channel_id=1, source_target_pairs={{0,1},{1,0},{2,3},{3,2},{4,5},{5,4},{6,7},{7,6},{8,9},{9,8},{10,11... | collective-permute-start | bytes 786440 | tf_op jit(solution)/shard_map/ppermute | solution.py:24
  33.0 3.8 %collective-permute-start.4 = (f32[2,2,64,256]{3,2,1,0:T(8,128)S(1)}, f32[2,2,64,256]{3,2,1,0:T(8,128)S(1)}, u32[]{:S(2)}, u32[]{:S(2)}) collective-permute-start(f32[2,2,64,256]{3,2,1,0:T(8,128)S(1)} %get-tuple-element.240), channel_id=1, source_target_pairs={{0,16},{4,20},{8,24},{12,28},{16,0},{20,4},{24,8},{28,12},{1,17},{... | collective-permute-start | bytes 786440 | tf_op jit(solution)/shard_map/ppermute | solution.py:24
  37.5 12.9 %collective-permute-done.5.refs_3_ = f32[2,2,64,256]{3,2,1,0:T(8,128)S(1)} collective-permute-done((f32[2,2,64,256]{3,2,1,0:T(8,128)S(1)}, f32[2,2,64,256]{3,2,1,0:T(8,128)S(1)}, u32[]{:S(2)}, u32[]{:S(2)}) %collective-permute-start.5) | collective-permute-done | bytes 262176 | tf_op jit(solution)/shard_map/ppermute | solution.py:24
  50.3 4.7 %collective-permute-done.4.refs_2_ = f32[2,2,64,256]{3,2,1,0:T(8,128)S(1)} collective-permute-done((f32[2,2,64,256]{3,2,1,0:T(8,128)S(1)}, f32[2,2,64,256]{3,2,1,0:T(8,128)S(1)}, u32[]{:S(2)}, u32[]{:S(2)}) %collective-permute-start.4) | collective-permute-done | bytes 262176 | tf_op jit(solution)/shard_map/ppermute | solution.py:24
  57.8 10.8 %collective-permute-done.15.refs_3_ = f32[4,2,2,32,256]{4,3,2,1,0:T(8,128)S(1)} collective-permute-done((f32[4,2,2,32,256]{4,3,2,1,0:T(8,128)S(1)}, f32[4,2,2,32,256]{4,3,2,1,0:T(8,128)S(1)}, u32[]{:S(2)}, u32[]{:S(2)}) %collective-permute-start.15) | collective-permute-done | bytes 524320 | tf_op jit(solution)/shard_map/ppermute | solution.py:24
  72.1 4.0 %collective-permute-start.20 = (f32[2,2,64,256]{3,2,1,0:T(8,128)S(1)}, f32[2,2,64,256]{3,2,1,0:T(8,128)S(1)}, u32[]{:S(2)}, u32[]{:S(2)}) collective-permute-start(f32[2,2,64,256]{3,2,1,0:T(8,128)S(1)} %get-tuple-element.236), channel_id=1, source_target_pairs={{0,16},{4,20},{8,24},{12,28},{16,0},{20,4},{24,8},{28,12},{1,17},{... | collective-permute-start | bytes 786440 | tf_op jit(solution)/shard_map/ppermute | solution.py:24
  76.2 9.2 %collective-permute-done.21.refs_3_ = f32[2,2,64,256]{3,2,1,0:T(8,128)S(1)} collective-permute-done((f32[2,2,64,256]{3,2,1,0:T(8,128)S(1)}, f32[2,2,64,256]{3,2,1,0:T(8,128)S(1)}, u32[]{:S(2)}, u32[]{:S(2)}) %collective-permute-start.21) | collective-permute-done | bytes 262176 | tf_op jit(solution)/shard_map/ppermute | solution.py:24
  85.4 8.0 %collective-permute-done.20.refs_2_ = f32[2,2,64,256]{3,2,1,0:T(8,128)S(1)} collective-permute-done((f32[2,2,64,256]{3,2,1,0:T(8,128)S(1)}, f32[2,2,64,256]{3,2,1,0:T(8,128)S(1)}, u32[]{:S(2)}, u32[]{:S(2)}) %collective-permute-start.20) | collective-permute-done | bytes 262176 | tf_op jit(solution)/shard_map/ppermute | solution.py:24
  95.4 2.8 %collective-permute-start.22 = (f32[4,2,2,32,256]{4,3,2,1,0:T(8,128)S(1)}, f32[4,2,2,32,256]{4,3,2,1,0:T(8,128)S(1)}, u32[]{:S(2)}, u32[]{:S(2)}) collective-permute-start(f32[4,2,2,32,256]{4,3,2,1,0:T(8,128)S(1)} %get-tuple-element.177.refs_2_), channel_id=1, source_target_pairs={{0,1},{1,0},{2,3},{3,2},{4,5},{5,4},{6,7},{7,6},{8,9},{9,8},{10,11... | collective-permute-start | bytes 1572872 | tf_op jit(solution)/shard_map/ppermute | solution.py:24
  98.8 1.8 dynamic-slice_bitcast_fusion.8
  102.1 4.0 %collective-permute-start.1 = (f32[2,1,64,256]{3,2,1,0:T(8,128)}, f32[2,1,64,256]{3,2,1,0:T(8,128)}, u32[]{:S(2)}, u32[]{:S(2)}) collective-permute-start(f32[2,1,64,256]{3,2,1,0:T(8,128)} %get-tuple-element.232), channel_id=1, source_target_pairs={{0,16},{4,20},{8,24},{12,28},{16,0},{20,4},{24,8},{28,12},{1,17},{... | collective-permute-start | bytes 393224 | tf_op jit(solution)/shard_map/ppermute | solution.py:24
  109.8 4.0 %collective-permute-done.1.refs_2_ = f32[2,1,64,256]{3,2,1,0:T(8,128)} collective-permute-done((f32[2,1,64,256]{3,2,1,0:T(8,128)}, f32[2,1,64,256]{3,2,1,0:T(8,128)}, u32[]{:S(2)}, u32[]{:S(2)}) %collective-permute-start.1) | collective-permute-done | bytes 131104 | tf_op jit(solution)/shard_map/ppermute | solution.py:24
  121.1 13.3 %collective-permute-done.24.refs_3_ = f32[4,2,1,32,256]{4,3,2,1,0:T(8,128)S(1)} collective-permute-done((f32[4,2,1,32,256]{4,3,2,1,0:T(8,128)S(1)}, f32[4,2,1,32,256]{4,3,2,1,0:T(8,128)S(1)}, u32[]{:S(2)}, u32[]{:S(2)}) %collective-permute-start.24) | collective-permute-done | bytes 262176 | tf_op jit(solution)/shard_map/ppermute | solution.py:24
  135.9 2.8 %collective-permute-start.32 = (f32[4,2,2,32,256]{4,3,2,1,0:T(8,128)S(1)}, f32[4,2,2,32,256]{4,3,2,1,0:T(8,128)S(1)}, u32[]{:S(2)}, u32[]{:S(2)}) collective-permute-start(f32[4,2,2,32,256]{4,3,2,1,0:T(8,128)S(1)} %get-tuple-element.209.refs_2_), channel_id=1, source_target_pairs={{0,1},{1,0},{2,3},{3,2},{4,5},{5,4},{6,7},{7,6},{8,9},{9,8},{10,11... | collective-permute-start | bytes 1572872 | tf_op jit(solution)/shard_map/ppermute | solution.py:24
  140.5 2.6 %collective-permute-start.45 = (f32[2,1,64,256]{3,2,1,0:T(8,128)S(1)}, f32[2,1,64,256]{3,2,1,0:T(8,128)S(1)}, u32[]{:S(2)}, u32[]{:S(2)}) collective-permute-start(f32[2,1,64,256]{3,2,1,0:T(8,128)S(1)} %copy-done.9), channel_id=1, source_target_pairs={{0,8},{4,12},{8,0},{12,4},{16,24},{20,28},{24,16},{28,20},{1,9},{5... | collective-permute-start | bytes 393224 | tf_op jit(solution)/shard_map/ppermute | solution.py:24
  143.3 2.8 %collective-permute-done.45.e1_ref = f32[2,1,64,256]{3,2,1,0:T(8,128)S(1)} collective-permute-done((f32[2,1,64,256]{3,2,1,0:T(8,128)S(1)}, f32[2,1,64,256]{3,2,1,0:T(8,128)S(1)}, u32[]{:S(2)}, u32[]{:S(2)}) %collective-permute-start.45) | collective-permute-done | bytes 131104 | tf_op jit(solution)/shard_map/ppermute | solution.py:24
  147.3 2.1 collective-permute-start.43
  154.0 25.4 %collective-permute-done.46.e2_ref = f32[2,1,64,256]{3,2,1,0:T(8,128)S(1)} collective-permute-done((f32[2,1,64,256]{3,2,1,0:T(8,128)S(1)}, f32[2,1,64,256]{3,2,1,0:T(8,128)S(1)}, u32[]{:S(2)}, u32[]{:S(2)}) %collective-permute-start.46) | collective-permute-done | bytes 131104 | tf_op jit(solution)/shard_map/ppermute | solution.py:24
  179.3 2.3 %collective-permute-start.39 = (f32[2,2,64,256]{3,2,1,0:T(8,128)S(1)}, f32[2,2,64,256]{3,2,1,0:T(8,128)S(1)}, u32[]{:S(2)}, u32[]{:S(2)}) collective-permute-start(f32[2,2,64,256]{3,2,1,0:T(8,128)S(1)} %get-tuple-element.214), channel_id=1, source_target_pairs={{0,8},{4,12},{8,0},{12,4},{16,24},{20,28},{24,16},{28,20},{1,9},{5... | collective-permute-start | bytes 786440 | tf_op jit(solution)/shard_map/ppermute | solution.py:24
  184.0 3.1 %collective-permute-start.34 = (f32[4,2,1,32,256]{4,3,2,1,0:T(8,128)S(1)}, f32[4,2,1,32,256]{4,3,2,1,0:T(8,128)S(1)}, u32[]{:S(2)}, u32[]{:S(2)}) collective-permute-start(f32[4,2,1,32,256]{4,3,2,1,0:T(8,128)S(1)} %get-tuple-element.223.refs_2_), channel_id=1, source_target_pairs={{0,1},{1,0},{2,3},{3,2},{4,5},{5,4},{6,7},{7,6},{8,9},{9,8},{10,11... | collective-permute-start | bytes 786440 | tf_op jit(solution)/shard_map/ppermute | solution.py:24
  187.3 1.9 finish.4.rest_0_
  189.2 3.5 %finish.5.rest_0_ = f32[2,6,256,256]{3,2,1,0:T(8,128)} custom-call(bf16[2,512,512]{2,1,0:T(8,128)(2,1)S(1)} %pad_maximum_fusion.1.right_ref, bf16[2,512,512]{2,1,0:T(8,128)(2,1)S(1)} %pad_maximum_fusion.3.left_ref, f32[2,2,64,256]{3,2,1,0:T(8,128)S(1)} %get-tuple-element.181.e0_ref, ...), custom_call_target="tpu_custom_call", output_to_operand_aliasing={{}: (6, {})} | custom-call | flops 1610612736 | bytes 2097152 | tf_op jit(solution)/shard_map/finish/pallas_call | solution.py:208
  193.4 2.7 %collective-permute-start.36 = (f32[2,1,64,256]{3,2,1,0:T(8,128)S(1)}, f32[2,1,64,256]{3,2,1,0:T(8,128)S(1)}, u32[]{:S(2)}, u32[]{:S(2)}) collective-permute-start(f32[2,1,64,256]{3,2,1,0:T(8,128)S(1)} %get-tuple-element.228), channel_id=1, source_target_pairs={{0,8},{4,12},{8,0},{12,4},{16,24},{20,28},{24,16},{28,20},{1,9},{5... | collective-permute-start | bytes 393224 | tf_op jit(solution)/shard_map/ppermute | solution.py:24
  197.4 14.0 %collective-permute-done.41.e3_ref = f32[2,2,64,256]{3,2,1,0:T(8,128)S(1)} collective-permute-done((f32[2,2,64,256]{3,2,1,0:T(8,128)S(1)}, f32[2,2,64,256]{3,2,1,0:T(8,128)S(1)}, u32[]{:S(2)}, u32[]{:S(2)}) %collective-permute-start.41) | collective-permute-done | bytes 262176 | tf_op jit(solution)/shard_map/ppermute | solution.py:24
  211.4 3.5 %finish.6.rest_0_ = f32[2,6,256,256]{3,2,1,0:T(8,128)} custom-call(bf16[2,512,512]{2,1,0:T(8,128)(2,1)S(1)} %pad_maximum_fusion.1.right_ref, bf16[2,512,512]{2,1,0:T(8,128)(2,1)S(1)} %pad_maximum_fusion.3.left_ref, f32[2,2,64,256]{3,2,1,0:T(8,128)S(1)} %get-tuple-element.213.e0_ref, ...), custom_call_target="tpu_custom_call", output_to_operand_aliasing={{}: (6, {})} | custom-call | flops 1610612736 | bytes 2097152 | tf_op jit(solution)/shard_map/finish/pallas_call | solution.py:208
  215.0 1.8 collective-permute-done.38.e3_ref
  216.7 1.9 finish.7
  (122 shorter events, 45.5 us)
Async XLA Ops:
  1.5 10.8 %collective-permute-start.7 = (f32[2,1,64,256]{3,2,1,0:T(8,128)S(1)}, f32[2,1,64,256]{3,2,1,0:T(8,128)S(1)}, u32[]{:S(2)}, u32[]{:S(2)}) collective-permute-start(f32[2,1,64,256]{3,2,1,0:T(8,128)S(1)} %get-tuple-element.244), channel_id=1, source_target_pairs={{0,16},{4,20},{8,24},{12,28},{16,0},{20,4},{24,8},{28,12},{1,17},{... | collective-permute-start | bytes 393224 | tf_op jit(solution)/shard_map/ppermute | solution.py:24
  31.6 18.7 %collective-permute-start.5 = (f32[2,2,64,256]{3,2,1,0:T(8,128)S(1)}, f32[2,2,64,256]{3,2,1,0:T(8,128)S(1)}, u32[]{:S(2)}, u32[]{:S(2)}) collective-permute-start(f32[2,2,64,256]{3,2,1,0:T(8,128)S(1)} %get-tuple-element.239), channel_id=1, source_target_pairs={{0,24},{4,28},{8,16},{12,20},{16,8},{20,12},{24,0},{28,4},{1,25},{... | collective-permute-start | bytes 786440 | tf_op jit(solution)/shard_map/ppermute | solution.py:24
  33.0 22.1 %collective-permute-start.4 = (f32[2,2,64,256]{3,2,1,0:T(8,128)S(1)}, f32[2,2,64,256]{3,2,1,0:T(8,128)S(1)}, u32[]{:S(2)}, u32[]{:S(2)}) collective-permute-start(f32[2,2,64,256]{3,2,1,0:T(8,128)S(1)} %get-tuple-element.240), channel_id=1, source_target_pairs={{0,16},{4,20},{8,24},{12,28},{16,0},{20,4},{24,8},{28,12},{1,17},{... | collective-permute-start | bytes 786440 | tf_op jit(solution)/shard_map/ppermute | solution.py:24
  36.8 18.3 %collective-permute-start.3 = (f32[2,2,64,256]{3,2,1,0:T(8,128)S(1)}, f32[2,2,64,256]{3,2,1,0:T(8,128)S(1)}, u32[]{:S(2)}, u32[]{:S(2)}) collective-permute-start(f32[2,2,64,256]{3,2,1,0:T(8,128)S(1)} %get-tuple-element.241), channel_id=1, source_target_pairs={{0,8},{4,12},{8,0},{12,4},{16,24},{20,28},{24,16},{28,20},{1,9},{5... | collective-permute-start | bytes 786440 | tf_op jit(solution)/shard_map/ppermute | solution.py:24
  56.3 12.3 %collective-permute-start.15 = (f32[4,2,2,32,256]{4,3,2,1,0:T(8,128)S(1)}, f32[4,2,2,32,256]{4,3,2,1,0:T(8,128)S(1)}, u32[]{:S(2)}, u32[]{:S(2)}) collective-permute-start(f32[4,2,2,32,256]{4,3,2,1,0:T(8,128)S(1)} %get-tuple-element.159.refs_2_), channel_id=1, source_target_pairs={{0,4},{4,0},{8,12},{12,8},{16,20},{20,16},{24,28},{28,24},{1,5},{5... | collective-permute-start | bytes 1572872 | tf_op jit(solution)/shard_map/ppermute | solution.py:24
  56.6 12.0 %collective-permute-start.16 = (f32[4,2,2,32,256]{4,3,2,1,0:T(8,128)S(1)}, f32[4,2,2,32,256]{4,3,2,1,0:T(8,128)S(1)}, u32[]{:S(2)}, u32[]{:S(2)}) collective-permute-start(f32[4,2,2,32,256]{4,3,2,1,0:T(8,128)S(1)} %get-tuple-element.161.refs_4_), channel_id=1, source_target_pairs={{0,2},{1,3},{2,0},{3,1},{4,6},{5,7},{6,4},{7,5},{8,10},{9,11},{10,... | collective-permute-start | bytes 1572872 | tf_op jit(solution)/shard_map/ppermute | solution.py:24
  69.3 25.3 %collective-permute-start.17 = (f32[4,2,2,32,256]{4,3,2,1,0:T(8,128)S(1)}, f32[4,2,2,32,256]{4,3,2,1,0:T(8,128)S(1)}, u32[]{:S(2)}, u32[]{:S(2)}) collective-permute-start(f32[4,2,2,32,256]{4,3,2,1,0:T(8,128)S(1)} %get-tuple-element.171.refs_2_), channel_id=1, source_target_pairs={{0,2},{1,3},{2,0},{3,1},{4,6},{5,7},{6,4},{7,5},{8,10},{9,11},{10,... | collective-permute-start | bytes 1572872 | tf_op jit(solution)/shard_map/ppermute | solution.py:24
  70.6 24.1 %collective-permute-start.18 = (f32[4,2,2,32,256]{4,3,2,1,0:T(8,128)S(1)}, f32[4,2,2,32,256]{4,3,2,1,0:T(8,128)S(1)}, u32[]{:S(2)}, u32[]{:S(2)}) collective-permute-start(f32[4,2,2,32,256]{4,3,2,1,0:T(8,128)S(1)} %get-tuple-element.173.refs_4_), channel_id=1, source_target_pairs={{0,4},{4,0},{8,12},{12,8},{16,20},{20,16},{24,28},{28,24},{1,5},{5... | collective-permute-start | bytes 1572872 | tf_op jit(solution)/shard_map/ppermute | solution.py:24
  71.9 13.6 %collective-permute-start.21 = (f32[2,2,64,256]{3,2,1,0:T(8,128)S(1)}, f32[2,2,64,256]{3,2,1,0:T(8,128)S(1)}, u32[]{:S(2)}, u32[]{:S(2)}) collective-permute-start(f32[2,2,64,256]{3,2,1,0:T(8,128)S(1)} %get-tuple-element.235), channel_id=1, source_target_pairs={{0,24},{4,28},{8,16},{12,20},{16,8},{20,12},{24,0},{28,4},{1,25},{... | collective-permute-start | bytes 786440 | tf_op jit(solution)/shard_map/ppermute | solution.py:24
  72.1 21.4 %collective-permute-start.20 = (f32[2,2,64,256]{3,2,1,0:T(8,128)S(1)}, f32[2,2,64,256]{3,2,1,0:T(8,128)S(1)}, u32[]{:S(2)}, u32[]{:S(2)}) collective-permute-start(f32[2,2,64,256]{3,2,1,0:T(8,128)S(1)} %get-tuple-element.236), channel_id=1, source_target_pairs={{0,16},{4,20},{8,24},{12,28},{16,0},{20,4},{24,8},{28,12},{1,17},{... | collective-permute-start | bytes 786440 | tf_op jit(solution)/shard_map/ppermute | solution.py:24
  76.1 17.4 %collective-permute-start.19 = (f32[2,2,64,256]{3,2,1,0:T(8,128)S(1)}, f32[2,2,64,256]{3,2,1,0:T(8,128)S(1)}, u32[]{:S(2)}, u32[]{:S(2)}) collective-permute-start(f32[2,2,64,256]{3,2,1,0:T(8,128)S(1)} %get-tuple-element.237), channel_id=1, source_target_pairs={{0,8},{4,12},{8,0},{12,4},{16,24},{20,28},{24,16},{28,20},{1,9},{5... | collective-permute-start | bytes 786440 | tf_op jit(solution)/shard_map/ppermute | solution.py:24
  98.3 16.7 %collective-permute-start.26 = (f32[4,2,2,32,256]{4,3,2,1,0:T(8,128)S(1)}, f32[4,2,2,32,256]{4,3,2,1,0:T(8,128)S(1)}, u32[]{:S(2)}, u32[]{:S(2)}) collective-permute-start(f32[4,2,2,32,256]{4,3,2,1,0:T(8,128)S(1)} %get-tuple-element.191.refs_2_), channel_id=1, source_target_pairs={{0,4},{4,0},{8,12},{12,8},{16,20},{20,16},{24,28},{28,24},{1,5},{5... | collective-permute-start | bytes 1572872 | tf_op jit(solution)/shard_map/ppermute | solution.py:24
  98.5 16.5 %collective-permute-start.27 = (f32[4,2,2,32,256]{4,3,2,1,0:T(8,128)S(1)}, f32[4,2,2,32,256]{4,3,2,1,0:T(8,128)S(1)}, u32[]{:S(2)}, u32[]{:S(2)}) collective-permute-start(f32[4,2,2,32,256]{4,3,2,1,0:T(8,128)S(1)} %get-tuple-element.193.refs_4_), channel_id=1, source_target_pairs={{0,2},{1,3},{2,0},{3,1},{4,6},{5,7},{6,4},{7,5},{8,10},{9,11},{10,... | collective-permute-start | bytes 1572872 | tf_op jit(solution)/shard_map/ppermute | solution.py:24
  102.1 11.7 %collective-permute-start.1 = (f32[2,1,64,256]{3,2,1,0:T(8,128)}, f32[2,1,64,256]{3,2,1,0:T(8,128)}, u32[]{:S(2)}, u32[]{:S(2)}) collective-permute-start(f32[2,1,64,256]{3,2,1,0:T(8,128)} %get-tuple-element.232), channel_id=1, source_target_pairs={{0,16},{4,20},{8,24},{12,28},{16,0},{20,4},{24,8},{28,12},{1,17},{... | collective-permute-start | bytes 393224 | tf_op jit(solution)/shard_map/ppermute | solution.py:24
  115.8 19.2 %collective-permute-start.30 = (f32[4,2,2,32,256]{4,3,2,1,0:T(8,128)S(1)}, f32[4,2,2,32,256]{4,3,2,1,0:T(8,128)S(1)}, u32[]{:S(2)}, u32[]{:S(2)}) collective-permute-start(f32[4,2,2,32,256]{4,3,2,1,0:T(8,128)S(1)} %get-tuple-element.203.refs_2_), channel_id=1, source_target_pairs={{0,2},{1,3},{2,0},{3,1},{4,6},{5,7},{6,4},{7,5},{8,10},{9,11},{10,... | collective-permute-start | bytes 1572872 | tf_op jit(solution)/shard_map/ppermute | solution.py:24
  117.1 17.9 %collective-permute-start.31 = (f32[4,2,2,32,256]{4,3,2,1,0:T(8,128)S(1)}, f32[4,2,2,32,256]{4,3,2,1,0:T(8,128)S(1)}, u32[]{:S(2)}, u32[]{:S(2)}) collective-permute-start(f32[4,2,2,32,256]{4,3,2,1,0:T(8,128)S(1)} %get-tuple-element.205.refs_4_), channel_id=1, source_target_pairs={{0,4},{4,0},{8,12},{12,8},{16,20},{20,16},{24,28},{28,24},{1,5},{5... | collective-permute-start | bytes 1572872 | tf_op jit(solution)/shard_map/ppermute | solution.py:24
  119.4 15.0 %collective-permute-start.24 = (f32[4,2,1,32,256]{4,3,2,1,0:T(8,128)S(1)}, f32[4,2,1,32,256]{4,3,2,1,0:T(8,128)S(1)}, u32[]{:S(2)}, u32[]{:S(2)}) collective-permute-start(f32[4,2,1,32,256]{4,3,2,1,0:T(8,128)S(1)} %get-tuple-element.197.refs_2_), channel_id=1, source_target_pairs={{0,4},{4,0},{8,12},{12,8},{16,20},{20,16},{24,28},{28,24},{1,5},{5... | collective-permute-start | bytes 786440 | tf_op jit(solution)/shard_map/ppermute | solution.py:24
  119.7 14.7 %collective-permute-start.25 = (f32[4,2,1,32,256]{4,3,2,1,0:T(8,128)S(1)}, f32[4,2,1,32,256]{4,3,2,1,0:T(8,128)S(1)}, u32[]{:S(2)}, u32[]{:S(2)}) collective-permute-start(f32[4,2,1,32,256]{4,3,2,1,0:T(8,128)S(1)} %get-tuple-element.199.refs_4_), channel_id=1, source_target_pairs={{0,2},{1,3},{2,0},{3,1},{4,6},{5,7},{6,4},{7,5},{8,10},{9,11},{10,... | collective-permute-start | bytes 786440 | tf_op jit(solution)/shard_map/ppermute | solution.py:24
  135.9 14.4 %collective-permute-start.32 = (f32[4,2,2,32,256]{4,3,2,1,0:T(8,128)S(1)}, f32[4,2,2,32,256]{4,3,2,1,0:T(8,128)S(1)}, u32[]{:S(2)}, u32[]{:S(2)}) collective-permute-start(f32[4,2,2,32,256]{4,3,2,1,0:T(8,128)S(1)} %get-tuple-element.209.refs_2_), channel_id=1, source_target_pairs={{0,1},{1,0},{2,3},{3,2},{4,5},{5,4},{6,7},{7,6},{8,9},{9,8},{10,11... | collective-permute-start | bytes 1572872 | tf_op jit(solution)/shard_map/ppermute | solution.py:24
  138.6 13.0 %collective-permute-start.33 = (f32[4,2,2,32,256]{4,3,2,1,0:T(8,128)S(1)}, f32[4,2,2,32,256]{4,3,2,1,0:T(8,128)S(1)}, u32[]{:S(2)}, u32[]{:S(2)}) collective-permute-start(f32[4,2,2,32,256]{4,3,2,1,0:T(8,128)S(1)} %get-tuple-element.211.refs_4_), channel_id=1, source_target_pairs={{0,1},{1,0},{2,3},{3,2},{4,5},{5,4},{6,7},{7,6},{8,9},{9,8},{10,11... | collective-permute-start | bytes 1572872 | tf_op jit(solution)/shard_map/ppermute | solution.py:24
  139.1 10.3 %collective-permute-start.29 = (f32[4,2,1,32,256]{4,3,2,1,0:T(8,128)S(1)}, f32[4,2,1,32,256]{4,3,2,1,0:T(8,128)S(1)}, u32[]{:S(2)}, u32[]{:S(2)}) collective-permute-start(f32[4,2,1,32,256]{4,3,2,1,0:T(8,128)S(1)} %get-tuple-element.219.refs_4_), channel_id=1, source_target_pairs={{0,4},{4,0},{8,12},{12,8},{16,20},{20,16},{24,28},{28,24},{1,5},{5... | collective-permute-start | bytes 786440 | tf_op jit(solution)/shard_map/ppermute | solution.py:24
  146.1 37.2 %collective-permute-start.42 = (f32[2,2,64,256]{3,2,1,0:T(8,128)S(1)}, f32[2,2,64,256]{3,2,1,0:T(8,128)S(1)}, u32[]{:S(2)}, u32[]{:S(2)}) collective-permute-start(f32[2,2,64,256]{3,2,1,0:T(8,128)S(1)} %get-tuple-element.182), channel_id=1, source_target_pairs={{0,8},{4,12},{8,0},{12,4},{16,24},{20,28},{24,16},{28,20},{1,9},{5... | collective-permute-start | bytes 786440 | tf_op jit(solution)/shard_map/ppermute | solution.py:24
  147.3 36.7 %collective-permute-start.43 = (f32[2,2,64,256]{3,2,1,0:T(8,128)S(1)}, f32[2,2,64,256]{3,2,1,0:T(8,128)S(1)}, u32[]{:S(2)}, u32[]{:S(2)}) collective-permute-start(f32[2,2,64,256]{3,2,1,0:T(8,128)S(1)} %get-tuple-element.183), channel_id=1, source_target_pairs={{0,16},{4,20},{8,24},{12,28},{16,0},{20,4},{24,8},{28,12},{1,17},{... | collective-permute-start | bytes 786440 | tf_op jit(solution)/shard_map/ppermute | solution.py:24
  149.4 37.7 %collective-permute-start.44 = (f32[2,2,64,256]{3,2,1,0:T(8,128)S(1)}, f32[2,2,64,256]{3,2,1,0:T(8,128)S(1)}, u32[]{:S(2)}, u32[]{:S(2)}) collective-permute-start(f32[2,2,64,256]{3,2,1,0:T(8,128)S(1)} %get-tuple-element.184), channel_id=1, source_target_pairs={{0,24},{4,28},{8,16},{12,20},{16,8},{20,12},{24,0},{28,4},{1,25},{... | collective-permute-start | bytes 786440 | tf_op jit(solution)/shard_map/ppermute | solution.py:24
  150.2 29.1 %collective-permute-start.46 = (f32[2,1,64,256]{3,2,1,0:T(8,128)S(1)}, f32[2,1,64,256]{3,2,1,0:T(8,128)S(1)}, u32[]{:S(2)}, u32[]{:S(2)}) collective-permute-start(f32[2,1,64,256]{3,2,1,0:T(8,128)S(1)} %copy-done.7), channel_id=1, source_target_pairs={{0,16},{4,20},{8,24},{12,28},{16,0},{20,4},{24,8},{28,12},{1,17},{... | collective-permute-start | bytes 393224 | tf_op jit(solution)/shard_map/ppermute | solution.py:24
  151.6 31.6 %collective-permute-start.47 = (f32[2,1,64,256]{3,2,1,0:T(8,128)S(1)}, f32[2,1,64,256]{3,2,1,0:T(8,128)S(1)}, u32[]{:S(2)}, u32[]{:S(2)}) collective-permute-start(f32[2,1,64,256]{3,2,1,0:T(8,128)S(1)} %copy-done.5), channel_id=1, source_target_pairs={{0,24},{4,28},{8,16},{12,20},{16,8},{20,12},{24,0},{28,4},{1,25},{... | collective-permute-start | bytes 393224 | tf_op jit(solution)/shard_map/ppermute | solution.py:24
  179.3 17.4 %collective-permute-start.39 = (f32[2,2,64,256]{3,2,1,0:T(8,128)S(1)}, f32[2,2,64,256]{3,2,1,0:T(8,128)S(1)}, u32[]{:S(2)}, u32[]{:S(2)}) collective-permute-start(f32[2,2,64,256]{3,2,1,0:T(8,128)S(1)} %get-tuple-element.214), channel_id=1, source_target_pairs={{0,8},{4,12},{8,0},{12,4},{16,24},{20,28},{24,16},{28,20},{1,9},{5... | collective-permute-start | bytes 786440 | tf_op jit(solution)/shard_map/ppermute | solution.py:24
  183.2 14.2 %collective-permute-start.40 = (f32[2,2,64,256]{3,2,1,0:T(8,128)S(1)}, f32[2,2,64,256]{3,2,1,0:T(8,128)S(1)}, u32[]{:S(2)}, u32[]{:S(2)}) collective-permute-start(f32[2,2,64,256]{3,2,1,0:T(8,128)S(1)} %get-tuple-element.215), channel_id=1, source_target_pairs={{0,16},{4,20},{8,24},{12,28},{16,0},{20,4},{24,8},{28,12},{1,17},{... | collective-permute-start | bytes 786440 | tf_op jit(solution)/shard_map/ppermute | solution.py:24
  183.2 28.2 %collective-permute-start.41 = (f32[2,2,64,256]{3,2,1,0:T(8,128)S(1)}, f32[2,2,64,256]{3,2,1,0:T(8,128)S(1)}, u32[]{:S(2)}, u32[]{:S(2)}) collective-permute-start(f32[2,2,64,256]{3,2,1,0:T(8,128)S(1)} %get-tuple-element.216), channel_id=1, source_target_pairs={{0,24},{4,28},{8,16},{12,20},{16,8},{20,12},{24,0},{28,4},{1,25},{... | collective-permute-start | bytes 786440 | tf_op jit(solution)/shard_map/ppermute | solution.py:24
  193.4 21.5 %collective-permute-start.36 = (f32[2,1,64,256]{3,2,1,0:T(8,128)S(1)}, f32[2,1,64,256]{3,2,1,0:T(8,128)S(1)}, u32[]{:S(2)}, u32[]{:S(2)}) collective-permute-start(f32[2,1,64,256]{3,2,1,0:T(8,128)S(1)} %get-tuple-element.228), channel_id=1, source_target_pairs={{0,8},{4,12},{8,0},{12,4},{16,24},{20,28},{24,16},{28,20},{1,9},{5... | collective-permute-start | bytes 393224 | tf_op jit(solution)/shard_map/ppermute | solution.py:24
  196.1 18.8 %collective-permute-start.37 = (f32[2,1,64,256]{3,2,1,0:T(8,128)S(1)}, f32[2,1,64,256]{3,2,1,0:T(8,128)S(1)}, u32[]{:S(2)}, u32[]{:S(2)}) collective-permute-start(f32[2,1,64,256]{3,2,1,0:T(8,128)S(1)} %get-tuple-element.229), channel_id=1, source_target_pairs={{0,16},{4,20},{8,24},{12,28},{16,0},{20,4},{24,8},{28,12},{1,17},{... | collective-permute-start | bytes 393224 | tf_op jit(solution)/shard_map/ppermute | solution.py:24
  196.7 20.1 %collective-permute-start.38 = (f32[2,1,64,256]{3,2,1,0:T(8,128)S(1)}, f32[2,1,64,256]{3,2,1,0:T(8,128)S(1)}, u32[]{:S(2)}, u32[]{:S(2)}) collective-permute-start(f32[2,1,64,256]{3,2,1,0:T(8,128)S(1)} %get-tuple-element.230), channel_id=1, source_target_pairs={{0,24},{4,28},{8,16},{12,20},{16,8},{20,12},{24,0},{28,4},{1,25},{... | collective-permute-start | bytes 393224 | tf_op jit(solution)/shard_map/ppermute | solution.py:24
  (27 other events, 347.6 us)
